TPU v7x, 32 devices: a whole 2x2x4 slice. The times are simulated.
32 devices in a mesh: grp: 2 (over x), wave: 16 (over z, y, core).
Axes of the slice: x: 2, y: 2, z: 4, core: 2. Of those that a mesh axis runs over, the one named last changes fastest.
Arguments:
- north_rows: bfloat16 [2560, 128, 274], P(('grp', 'wave')), parts along dimension 0, may hold values from -6 to 6
- south_rows: bfloat16 [2560, 128, 274], P(('grp', 'wave')), parts along dimension 0, may hold values from -6 to 6
- lon_counts: int32 [1280], replicated, may hold values from 20 to 5148, as said below
- slot_wave: int32 [128], replicated, may hold values from 0 to 2559, as said below
- legendre: bfloat16 [128, 1280, 1280], P('wave'), may hold values from -0.15625 to 0.15625
- mode_rates: float32 [137], replicated, may hold values from 0.05 to 20
- to_modes: bfloat16 [137, 137], replicated, may hold values from -0.5 to 0.5
- from_modes: bfloat16 [137, 137], replicated, may hold values from -0.5 to 0.5
Outputs:
- spec_state: bfloat16 [256, 1280, 274], P(('grp', 'wave')), parts along dimension 0
- new_rows: bfloat16 [2560, 128, 274], P(('grp', 'wave')), parts along dimension 0
There are 2 independent parts, one for each index of `grp`. A program takes and returns all parts, laid end to end along the dimension named above; an argument that names none is the same for every part. Nothing has to cross between parts.
Inputs may be any that keep to these rules, and one draw needn't show every extreme that they name: Wavenumber m is present in latitude row j only if 2 m is below lon_counts[j]. `slot_wave`: distinct zonal wavenumbers.
All inputs are finite; a program needn't handle non-finite values.
Results may differ from a plain program's by a relative error of at most 0.0065.
Values may be sent and summed in bfloat16 or wider, within the bound.
A program may use at most 192 MiB of HBM per device.

v0:
```python
import jax
import jax.numpy as jnp
from jax import lax
from jax.sharding import PartitionSpec as P

NMAX = 2559


def vertical_step(direct, own_waves, mode_rates, to_modes, from_modes):
    slot_count, row_total, channels = direct.shape
    levels = to_modes.shape[0]
    modal_part = jnp.dot(direct.reshape(-1, levels), to_modes, preferred_element_type=jnp.float32)
    modal_part = modal_part.reshape(slot_count, row_total, 2, levels)
    degree = own_waves[:, None] + 2 * jnp.arange(row_total, dtype=jnp.int32)[None, :]
    degree_f = degree.astype(jnp.float32)
    scaled_degree = degree_f * (degree_f + 1.0) / float(NMAX * (NMAX + 1))
    divisor = 1.0 + mode_rates[None, None, None, :] * scaled_degree[:, :, None, None]
    scaled = (modal_part / divisor).astype(jnp.bfloat16).reshape(-1, levels)
    result = jnp.dot(scaled, from_modes, preferred_element_type=jnp.float32)
    result = result.reshape(slot_count, row_total, channels)
    return jnp.where((degree <= NMAX)[:, :, None], result, 0.0).astype(jnp.bfloat16)


def per_device(
    north_rows, south_rows, lon_counts, slot_wave, legendre, mode_rates, to_modes, from_modes
):
    lat_dev = north_rows.shape[0]
    slot_dev, row_total, lat_total = legendre.shape
    my_index = lax.axis_index("wave")
    own_waves = lax.dynamic_slice_in_dim(slot_wave, my_index * slot_dev, slot_dev)
    live_own = 2 * own_waves[None, :] < lon_counts[:, None]
    local_counts = lax.dynamic_slice_in_dim(lon_counts, my_index * lat_dev, lat_dev)
    live_here = 2 * slot_wave[None, :] < local_counts[:, None]
    summed = north_rows.astype(jnp.float32) + south_rows.astype(jnp.float32)
    sym_here = jnp.where(live_here[:, :, None], summed, 0.0).astype(jnp.bfloat16)
    columns = lax.all_to_all(sym_here, "wave", split_axis=1, concat_axis=0, tiled=True)
    direct = jnp.einsum(
        "snj,jsc->snc", legendre, columns, preferred_element_type=jnp.float32
    ).astype(jnp.bfloat16)
    spec_state = vertical_step(direct, own_waves, mode_rates, to_modes, from_modes)
    returned = jnp.einsum("snj,snc->jsc", legendre, spec_state, preferred_element_type=jnp.float32)
    returned = jnp.where(live_own[:, :, None], returned, 0.0).astype(jnp.bfloat16)
    new_rows = lax.all_to_all(returned, "wave", split_axis=0, concat_axis=1, tiled=True)
    return (spec_state, new_rows)


def solution(mesh):
    in_specs = (
        P(("grp", "wave"), None, None),
        P(("grp", "wave"), None, None),
        P(),
        P(),
        P("wave", None, None),
        P(),
        P(),
        P(),
    )
    out_specs = (P(("grp", "wave"), None, None), P(("grp", "wave"), None, None))
    return jax.shard_map(
        per_device, mesh=mesh, in_specs=in_specs, out_specs=out_specs, check_vma=False
    )
```

profile of v0, /device:TPU:15, one launch (start us, length us, event | category | flops | bytes accessed | tf_op | source)
XLA Modules:
  0.0 580.0 jit_solution(6979879642193113835)
XLA Ops:
  0.7 11.0 %copy.45 = bf16[80,128,274]{2,0,1:T(8,128)(2,1)} copy(bf16[80,128,274]{1,0,2:T(8,128)(2,1)} %param.9) | data formatting | bytes 11223040 | tf_op args[1]
  11.6 11.0 %copy.44 = bf16[80,128,274]{2,0,1:T(8,128)(2,1)} copy(bf16[80,128,274]{1,0,2:T(8,128)(2,1)} %param.8) | data formatting | bytes 11223040 | tf_op args[0]
  22.9 9.6 %select_convert_fusion.1 = bf16[80,128,274]{2,0,1:T(8,128)(2,1)} fusion(bf16[80,128,274]{2,0,1:T(8,128)(2,1)} %copy.45, bf16[80,128,274]{2,0,1:T(8,128)(2,1)} %copy.44, pred[80,128]{0,1:T(8,128)(4,1)S(1)} %broadcast_compare_fusion), kind=kLoop, calls=%fused_computation.1 | loop fusion | flops 14028800 | bytes 16844800 | tf_op jit(solution)/shard_map/convert_element_type | solution.py:35
  32.5 6.7 %all-to-all-start = ((bf16[80,128,274]{2,0,1:T(8,128)(2,1)}), bf16[80,128,274]{2,0,1:T(8,128)(2,1)}, u32[]{:S(2)}, u32[]{:S(2)}) async-start(bf16[80,128,274]{2,0,1:T(8,128)(2,1)} %select_convert_fusion.1), calls=%async_computation | async-start | bytes 15728640 | tf_op jit(solution)/shard_map/all_to_all | solution.py:36
  39.5 3.2 multiply_add_fusion
  42.7 167.6 %all-to-all-done = bf16[80,128,274]{2,0,1:T(8,128)(2,1)} async-done(((bf16[80,128,274]{2,0,1:T(8,128)(2,1)}), bf16[80,128,274]{2,0,1:T(8,128)(2,1)}, u32[]{:S(2)}, u32[]{:S(2)}) %all-to-all-start) | async-done | bytes 5611552 | tf_op jit(solution)/shard_map/all_to_all | solution.py:36
  210.3 14.5 %copy.65 = bf16[16,80,8,274]{1,0,3,2:T(8,128)(2,1)} copy(bf16[16,80,8,274]{3,1,2,0:T(8,128)(2,1)} %bitcast.2) | data formatting | bytes 11223040 | tf_op jit(solution)/shard_map/all_to_all | solution.py:36
  224.8 13.2 %reshape.146 = bf16[1280,8,274]{0,2,1:T(8,128)(2,1)} reshape(bf16[16,80,8,274]{1,0,3,2:T(8,128)(2,1)} %copy.65) | data formatting | bytes 11223040 | tf_op jit(solution)/shard_map/all_to_all | solution.py:36
  238.0 25.7 %convert_bitcast_fusion = bf16[8,1280,274]{1,2,0:T(8,128)(2,1)} fusion(bf16[1280,8,274]{0,2,1:T(8,128)(2,1)} %reshape.146, bf16[8,1280,1280]{2,1,0:T(8,128)(2,1)} %param.12), kind=kOutput, calls=%fused_computation.8 | convolution fusion | flops 7185551360 | bytes 37437440 | tf_op jit(solution)/shard_map/snj,jsc->snc/dot_general | solution.py:37
  263.7 3.7 copy.49
  267.4 6.4 %divide_convert_fusion = bf16[8,1280,2,137]{1,3,2,0:T(8,128)(2,1)} fusion(bf16[8,1280,2,137]{1,0,3,2:T(8,128)(2,1)S(1)} %bitcast.31, f32[8,1280,137]{1,2,0:T(8,128)} %multiply_add_fusion, bf16[137,137]{1,0:T(8,128)(2,1)S(1)} %copy-done), kind=kOutput, calls=%fused_computation.2 | convolution fusion | flops 774389760 | bytes 16872098 | tf_op jit(solution)/shard_map/dot_general | solution.py:12
  273.8 25.2 %copy.52 = bf16[8,1280,2,137]{3,2,1,0:T(2,128)(2,1)} copy(bf16[8,1280,2,137]{1,3,2,0:T(8,128)(2,1)} %divide_convert_fusion) | data formatting | bytes 11223040 | tf_op jit(solution)/shard_map/convert_element_type | solution.py:18
  299.1 18.9 %reshape.143 = bf16[20480,137]{1,0:T(8,128)(2,1)} reshape(bf16[8,1280,2,137]{3,2,1,0:T(2,128)(2,1)} %copy.52) | data formatting | bytes 11223040 | tf_op jit(solution)/shard_map/reshape | solution.py:18
  318.0 10.8 %fusion.4 = bf16[20480,137]{1,0:T(8,128)(2,1)} fusion(bf16[20480,137]{1,0:T(8,128)(2,1)} %reshape.143, bf16[137,137]{1,0:T(8,128)(2,1)S(1)} %copy-done.2), kind=kOutput, calls=%fused_computation.19 | convolution fusion | flops 768778240 | bytes 11260578 | tf_op jit(solution)/shard_map/dot_general | solution.py:19
  328.8 16.0 %reshape.144 = bf16[8,1280,274]{2,1,0:T(8,128)(2,1)} reshape(bf16[20480,137]{1,0:T(8,128)(2,1)} %fusion.4) | data formatting | bytes 11223040 | tf_op jit(solution)/shard_map/reshape | solution.py:20
  344.8 7.6 %select_convert_fusion = bf16[8,1280,274]{2,1,0:T(8,128)(2,1)} fusion(bf16[8,1280,274]{2,1,0:T(8,128)(2,1)} %reshape.144, pred[8,1280]{1,0:T(8,128)(4,1)S(1)} %add_compare_fusion), kind=kLoop, calls=%fused_computation | loop fusion | flops 2805760 | bytes 11233280 | tf_op jit(solution)/shard_map/convert_element_type | solution.py:21
  352.4 16.3 %fusion.5 = bf16[8,274,1280]{2,1,0:T(8,128)(2,1)} fusion(bf16[8,1280,274]{2,1,0:T(8,128)(2,1)} %select_convert_fusion, bf16[8,1280,1280]{2,1,0:T(8,128)(2,1)} %param.12), kind=kOutput, calls=%fused_computation.20 | convolution fusion | flops 7182745600 | bytes 37437440 | tf_op jit(solution)/shard_map/snj,snc->jsc/dot_general | solution.py:41
  368.7 6.5 %fusion = bf16[1280,8,274]{0,1,2:T(8,128)(2,1)} fusion(bf16[8,274,1280]{2,1,0:T(8,128)(2,1)} %fusion.5, pred[1280,8]{0,1:T(8,128)(4,1)S(1)} %broadcast_compare_fusion.1), kind=kLoop, calls=%fused_computation.4 | loop fusion | flops 2805760 | bytes 11233280 | tf_op jit(solution)/shard_map/convert_element_type | solution.py:42
  375.2 10.9 %copy.56 = bf16[1280,8,274]{2,1,0:T(8,128)(2,1)} copy(bf16[1280,8,274]{0,1,2:T(8,128)(2,1)} %fusion) | data formatting | bytes 11223040 | tf_op jit(solution)/shard_map/convert_element_type | solution.py:42
  386.2 4.8 all-to-all-start.1
  391.0 10.1 %copy.59 = bf16[8,1280,274]{1,0,2:T(8,128)(2,1)} copy(bf16[8,1280,274]{2,1,0:T(8,128)(2,1)} %select_convert_fusion) | data formatting | bytes 11223040
  401.0 161.1 %all-to-all-done.1 = bf16[1280,8,274]{2,1,0:T(8,128)(2,1)} async-done(((bf16[1280,8,274]{2,1,0:T(8,128)(2,1)}), bf16[1280,8,274]{2,1,0:T(8,128)(2,1)}, u32[]{:S(2)}, u32[]{:S(2)}) %all-to-all-start.1) | async-done | bytes 5611552 | tf_op jit(solution)/shard_map/all_to_all | solution.py:43
  562.1 7.9 %copy.74 = bf16[80,16,8,274]{3,2,1,0:T(8,128)(2,1)} copy(bf16[80,16,8,274]{3,2,0,1:T(8,128)(2,1)} %bitcast.9) | data formatting | bytes 11223040 | tf_op jit(solution)/shard_map/all_to_all | solution.py:43
  570.0 10.0 %copy.60 = bf16[80,128,274]{1,0,2:T(8,128)(2,1)} copy(bf16[80,128,274]{2,1,0:T(8,128)(2,1)} %bitcast.30) | data formatting | bytes 11223040
  (20 shorter events, 0.5 us)
Async XLA Ops:
  0.6 266.8 %copy-start = (bf16[137,137]{1,0:T(8,128)(2,1)S(1)}, bf16[137,137]{1,0:T(8,128)(2,1)}, u32[]{:S(2)}) copy-start(bf16[137,137]{1,0:T(8,128)(2,1)} %param.14) | copy-start | bytes 112618
  11.6 11.1 %copy-start.5 = (s32[128]{0:T(128)S(1)}, s32[128]{0:T(128)}, u32[]{:S(2)}) copy-start(s32[128]{0:T(128)} %param.11) | copy-start | bytes 1540
  11.6 11.1 %copy-start.3 = (s32[1280]{0:T(1024)S(1)}, s32[1280]{0:T(1024)}, u32[]{:S(2)}) copy-start(s32[1280]{0:T(1024)} %param.10) | copy-start | bytes 15364
  32.5 7.0 %copy-start.4 = (f32[137]{0:T(256)S(1)}, f32[137]{0:T(256)}, u32[]{:S(2)}) copy-start(f32[137]{0:T(256)} %param.13) | copy-start | bytes 1648
  32.5 177.8 %all-to-all-start = ((bf16[80,128,274]{2,0,1:T(8,128)(2,1)}), bf16[80,128,274]{2,0,1:T(8,128)(2,1)}, u32[]{:S(2)}, u32[]{:S(2)}) async-start(bf16[80,128,274]{2,0,1:T(8,128)(2,1)} %select_convert_fusion.1), calls=%async_computation | async-start | bytes 15728640 | tf_op jit(solution)/shard_map/all_to_all | solution.py:36
  299.1 18.9 %copy-start.2 = (bf16[137,137]{1,0:T(8,128)(2,1)S(1)}, bf16[137,137]{1,0:T(8,128)(2,1)}, u32[]{:S(2)}) copy-start(bf16[137,137]{1,0:T(8,128)(2,1)} %param.15) | copy-start | bytes 112618
  386.2 175.9 %all-to-all-start.1 = ((bf16[1280,8,274]{2,1,0:T(8,128)(2,1)}), bf16[1280,8,274]{2,1,0:T(8,128)(2,1)}, u32[]{:S(2)}, u32[]{:S(2)}) async-start(bf16[1280,8,274]{2,1,0:T(8,128)(2,1)} %copy.56), calls=%async_computation.1 | async-start | bytes 15728640 | tf_op jit(solution)/shard_map/all_to_all | solution.py:43
  562.1 17.9 %copy-start.1 = (bf16[137,137]{1,0:T(8,128)(2,1)S(1)}, bf16[137,137]{1,0:T(8,128)(2,1)}, u32[]{:S(2)}) copy-start(bf16[137,137]{1,0:T(8,128)(2,1)} %param.14) | copy-start | bytes 112618
where the time goes:
time: 584 us; the launch traced here: 580 us
  waiting for transfers between devices  329 us (56%)
  local copies, waits for them, and re-layouts  153 us (26%)
  matrix products  59.3 us (10%)
  other arithmetic  27.3 us (5%)
  starting transfers between devices  11.4 us (2%)
    all_to_all x1, waiting for transfers between devices, per_device(): lax.all_to_all(sym_here, 'wave', split_axis=1, concat_axis=0, tiled=True)  168 us
    all_to_all x1, waiting for transfers between devices, per_device(): lax.all_to_all(returned, 'wave', split_axis=0, concat_axis=1, tiled=True)  161 us
    unnamed x16, local copies, waits for them, and re-layouts  42.2 us
    all_to_all x2, local copies, waits for them, and re-layouts, per_device(): lax.all_to_all(sym_here, 'wave', split_axis=1, concat_axis=0, tiled=True)  27.8 us
    dot_general x1, matrix products, per_device(): jnp.einsum('snj,jsc->snc', legendre, columns, preferred_element_type=jnp....  25.7 us
    convert_element_type x1, local copies, waits for them, and re-layouts, vertical_step(): scaled = (modal_part / divisor).astype(jnp.bfloat16).reshape(-1, levels)  25.2 us
    reshape x1, local copies, waits for them, and re-layouts, vertical_step(): scaled = (modal_part / divisor).astype(jnp.bfloat16).reshape(-1, levels)  18.9 us
    dot_general x1, matrix products, per_device(): jnp.einsum('snj,snc->jsc', legendre, spec_state, preferred_element_type=j...  16.3 us
  transfers between devices with their start and end apart: 2, of which 2 were waited for; matrix products, arithmetic and copies ran while one was open for 2% of the time, Pallas kernels for 0%

commit v1 on v0

--- a/solution.py
+++ b/solution.py
@@ -40,7 +40,10 @@
     spec_state = vertical_step(direct, own_waves, mode_rates, to_modes, from_modes)
     returned = jnp.einsum("snj,snc->jsc", legendre, spec_state, preferred_element_type=jnp.float32)
     returned = jnp.where(live_own[:, :, None], returned, 0.0).astype(jnp.bfloat16)
-    new_rows = lax.all_to_all(returned, "wave", split_axis=0, concat_axis=1, tiled=True)
+    new_rows = jnp.concatenate(
+        lax.all_to_all(jnp.stack(jnp.split(returned, lax.axis_size("wave"), axis=0)), "wave", 0, 0),
+        axis=1,
+    )
     return (spec_state, new_rows)
 
 

time: 584 us -> 607 us (1.039)
  local copies, waits for them, and re-layouts: 153 us -> 182 us
    unnamed x16 -> x33, local copies, waits for them, and re-layouts: 42.2 us -> 66.9 us
    another operation x0 -> x2, local copies, waits for them, and re-layouts: none -> 15.5 us  [per_device(): jnp.stack(jnp.split(returned, lax.axis_size('wave'), axis=0))]
    convert_element_type x1 -> x0, local copies, waits for them, and re-layouts: 10.9 us -> none  [per_device(): jnp.where(live_own[:, :, None], returned, 0.0).astype(jnp.bfloat16)]
    all_to_all x1 -> x0, local copies, waits for them, and re-layouts: 7.89 us -> none  [per_device(): lax.all_to_all(returned, 'wave', split_axis=0, concat_axis=1, tiled=True)]
    reshape x0 -> x1, local copies, waits for them, and re-layouts: none -> 7.88 us  [per_device(): jnp.concatenate(lax.all_to_all(jnp.stack(jnp.split(returned, lax.axis_siz...]
    convert_element_type x1 -> x0, other arithmetic: 6.5 us -> none  [per_device(): jnp.where(live_own[:, :, None], returned, 0.0).astype(jnp.bfloat16)]
where the time goes in v1:
time: 607 us; the launch traced here: 604 us
  waiting for transfers between devices  329 us (54%)
  local copies, waits for them, and re-layouts  182 us (30%)
  matrix products  59.3 us (10%)
  other arithmetic  21.5 us (4%)
  starting transfers between devices  11.4 us (2%)
    all_to_all x1, waiting for transfers between devices, per_device(): lax.all_to_all(sym_here, 'wave', split_axis=1, concat_axis=0, tiled=True)  168 us
    all_to_all x1, waiting for transfers between devices, per_device(): lax.all_to_all(jnp.stack(jnp.split(returned, lax.axis_size('wave'), axis=...  161 us
    unnamed x33, local copies, waits for them, and re-layouts  66.9 us
    all_to_all x2, local copies, waits for them, and re-layouts, per_device(): lax.all_to_all(sym_here, 'wave', split_axis=1, concat_axis=0, tiled=True)  27.8 us
    dot_general x1, matrix products, per_device(): jnp.einsum('snj,jsc->snc', legendre, columns, preferred_element_type=jnp....  25.7 us
    convert_element_type x1, local copies, waits for them, and re-layouts, vertical_step(): scaled = (modal_part / divisor).astype(jnp.bfloat16).reshape(-1, levels)  25.2 us
    reshape x1, local copies, waits for them, and re-layouts, vertical_step(): scaled = (modal_part / divisor).astype(jnp.bfloat16).reshape(-1, levels)  18.9 us
    dot_general x1, matrix products, per_device(): jnp.einsum('snj,snc->jsc', legendre, spec_state, preferred_element_type=j...  16.4 us
  transfers between devices with their start and end apart: 2, of which 2 were waited for; matrix products, arithmetic and copies ran while one was open for 2% of the time, Pallas kernels for 0%

profile of v1, /device:TPU:15, one launch (start us, length us, event | category | flops | bytes accessed | tf_op | source)
XLA Modules:
  0.0 603.5 jit_solution(16521682510964045879)
XLA Ops:
  1.3 11.0 %copy.39 = bf16[80,128,274]{2,0,1:T(8,128)(2,1)} copy(bf16[80,128,274]{1,0,2:T(8,128)(2,1)} %param.8) | data formatting | bytes 11223040 | tf_op args[0]
  12.3 11.0 %copy.40 = bf16[80,128,274]{2,0,1:T(8,128)(2,1)} copy(bf16[80,128,274]{1,0,2:T(8,128)(2,1)} %param.9) | data formatting | bytes 11223040 | tf_op args[1]
  23.5 9.6 %select_convert_fusion.1 = bf16[80,128,274]{2,0,1:T(8,128)(2,1)} fusion(bf16[80,128,274]{2,0,1:T(8,128)(2,1)} %copy.40, bf16[80,128,274]{2,0,1:T(8,128)(2,1)} %copy.39, pred[80,128]{0,1:T(8,128)(4,1)S(1)} %broadcast_compare_fusion), kind=kLoop, calls=%fused_computation.1 | loop fusion | flops 14028800 | bytes 16844800 | tf_op jit(solution)/shard_map/convert_element_type | solution.py:35
  33.1 6.7 %all-to-all-start = ((bf16[80,128,274]{2,0,1:T(8,128)(2,1)}), bf16[80,128,274]{2,0,1:T(8,128)(2,1)}, u32[]{:S(2)}, u32[]{:S(2)}) async-start(bf16[80,128,274]{2,0,1:T(8,128)(2,1)} %select_convert_fusion.1), calls=%async_computation | async-start | bytes 15728640 | tf_op jit(solution)/shard_map/all_to_all | solution.py:36
  40.1 3.2 multiply_add_fusion
  43.3 167.6 %all-to-all-done = bf16[80,128,274]{2,0,1:T(8,128)(2,1)} async-done(((bf16[80,128,274]{2,0,1:T(8,128)(2,1)}), bf16[80,128,274]{2,0,1:T(8,128)(2,1)}, u32[]{:S(2)}, u32[]{:S(2)}) %all-to-all-start) | async-done | bytes 5611552 | tf_op jit(solution)/shard_map/all_to_all | solution.py:36
  210.9 14.5 %copy.58 = bf16[16,80,8,274]{1,0,3,2:T(8,128)(2,1)} copy(bf16[16,80,8,274]{3,1,2,0:T(8,128)(2,1)} %bitcast.2) | data formatting | bytes 11223040 | tf_op jit(solution)/shard_map/all_to_all | solution.py:36
  225.4 13.3 %reshape.154 = bf16[1280,8,274]{0,2,1:T(8,128)(2,1)} reshape(bf16[16,80,8,274]{1,0,3,2:T(8,128)(2,1)} %copy.58) | data formatting | bytes 11223040 | tf_op jit(solution)/shard_map/all_to_all | solution.py:36
  238.7 25.7 %convert_bitcast_fusion = bf16[8,1280,274]{1,2,0:T(8,128)(2,1)} fusion(bf16[1280,8,274]{0,2,1:T(8,128)(2,1)} %reshape.154, bf16[8,1280,1280]{2,1,0:T(8,128)(2,1)} %param.12), kind=kOutput, calls=%fused_computation.8 | convolution fusion | flops 7185551360 | bytes 37437440 | tf_op jit(solution)/shard_map/snj,jsc->snc/dot_general | solution.py:37
  264.3 3.7 copy.44
  268.0 6.5 %divide_convert_fusion = bf16[8,1280,2,137]{1,3,2,0:T(8,128)(2,1)} fusion(bf16[8,1280,2,137]{1,0,3,2:T(8,128)(2,1)S(1)} %bitcast.92, f32[8,1280,137]{1,2,0:T(8,128)} %multiply_add_fusion, bf16[137,137]{1,0:T(8,128)(2,1)S(1)} %copy-done), kind=kOutput, calls=%fused_computation.2 | convolution fusion | flops 774389760 | bytes 16872098 | tf_op jit(solution)/shard_map/dot_general | solution.py:12
  274.5 25.2 %copy.47 = bf16[8,1280,2,137]{3,2,1,0:T(2,128)(2,1)} copy(bf16[8,1280,2,137]{1,3,2,0:T(8,128)(2,1)} %divide_convert_fusion) | data formatting | bytes 11223040 | tf_op jit(solution)/shard_map/convert_element_type | solution.py:18
  299.7 18.9 %reshape.149 = bf16[20480,137]{1,0:T(8,128)(2,1)} reshape(bf16[8,1280,2,137]{3,2,1,0:T(2,128)(2,1)} %copy.47) | data formatting | bytes 11223040 | tf_op jit(solution)/shard_map/reshape | solution.py:18
  318.6 10.8 %fusion.20 = bf16[20480,137]{1,0:T(8,128)(2,1)} fusion(bf16[20480,137]{1,0:T(8,128)(2,1)} %reshape.149, bf16[137,137]{1,0:T(8,128)(2,1)S(1)} %copy-done.3), kind=kOutput, calls=%fused_computation.51 | convolution fusion | flops 768778240 | bytes 11260578 | tf_op jit(solution)/shard_map/dot_general | solution.py:19
  329.4 16.0 %reshape.150 = bf16[8,1280,274]{2,1,0:T(8,128)(2,1)} reshape(bf16[20480,137]{1,0:T(8,128)(2,1)} %fusion.20) | data formatting | bytes 11223040 | tf_op jit(solution)/shard_map/reshape | solution.py:20
  345.4 7.6 %select_convert_fusion = bf16[8,1280,274]{2,1,0:T(8,128)(2,1)} fusion(bf16[8,1280,274]{2,1,0:T(8,128)(2,1)} %reshape.150, pred[8,1280]{1,0:T(8,128)(4,1)S(1)} %add_compare_fusion), kind=kLoop, calls=%fused_computation | loop fusion | flops 2805760 | bytes 11233280 | tf_op jit(solution)/shard_map/convert_element_type | solution.py:21
  353.0 16.4 %fusion = bf16[1280,8,274]{0,2,1:T(8,128)(2,1)} fusion(bf16[8,1280,274]{2,1,0:T(8,128)(2,1)} %select_convert_fusion, bf16[8,1280,1280]{2,1,0:T(8,128)(2,1)} %param.12, pred[1280,8]{0,1:T(8,128)(4,1)S(1)} %broadcast_compare_fusion.1), kind=kOutput, calls=%fused_computation.4 | convolution fusion | flops 7188357120 | bytes 37447680 | tf_op jit(solution)/shard_map/snj,snc->jsc/dot_general | solution.py:41
  371.4 2.3 fusion.16
  395.3 14.4 %copy.50 = bf16[16,80,8,274]{3,2,1,0:T(8,128)(2,1)} copy(bf16[16,80,8,274]{1,3,2,0:T(8,128)(2,1)} %fusion.2) | data formatting | bytes 11223040 | tf_op jit(solution)/shard_map/stack | solution.py:44
  409.7 4.8 all-to-all-start.1
  414.5 10.1 %copy.52 = bf16[8,1280,274]{1,0,2:T(8,128)(2,1)} copy(bf16[8,1280,274]{2,1,0:T(8,128)(2,1)} %select_convert_fusion) | data formatting | bytes 11223040
  424.5 161.1 %all-to-all-done.1 = bf16[16,80,8,274]{3,2,1,0:T(8,128)(2,1)} async-done(((bf16[16,80,8,274]{3,2,1,0:T(8,128)(2,1)}), bf16[16,80,8,274]{3,2,1,0:T(8,128)(2,1)}, u32[]{:S(2)}, u32[]{:S(2)}) %all-to-all-start.1) | async-done | bytes 5611552 | tf_op jit(solution)/shard_map/all_to_all | solution.py:44
  585.6 7.9 %copy_bitcast_fusion = bf16[80,128,274]{2,1,0:T(8,128)(2,1)} fusion(bf16[16,80,8,274]{3,2,1,0:T(8,128)(2,1)} %all-to-all-done.1), kind=kLoop, calls=%fused_computation.5 | loop fusion | bytes 11223040 | tf_op jit(solution)/shard_map/reshape | solution.py:43
  593.5 10.0 %copy.53 = bf16[80,128,274]{1,0,2:T(8,128)(2,1)} copy(bf16[80,128,274]{2,1,0:T(8,128)(2,1)} %copy_bitcast_fusion) | data formatting | bytes 11223040
  (37 shorter events, 24.8 us)
Async XLA Ops:
  0.6 267.4 %copy-start = (bf16[137,137]{1,0:T(8,128)(2,1)S(1)}, bf16[137,137]{1,0:T(8,128)(2,1)}, u32[]{:S(2)}) copy-start(bf16[137,137]{1,0:T(8,128)(2,1)} %param.14) | copy-start | bytes 112618
  12.3 11.0 %copy-start.4 = (s32[1280]{0:T(1024)S(1)}, s32[1280]{0:T(1024)}, u32[]{:S(2)}) copy-start(s32[1280]{0:T(1024)} %param.10) | copy-start | bytes 15364
  33.1 6.7 %copy-start.6 = (s32[128]{0:T(128)S(1)}, s32[128]{0:T(128)}, u32[]{:S(2)}) copy-start(s32[128]{0:T(128)} %param.11) | copy-start | bytes 1540
  33.1 7.0 %copy-start.5 = (f32[137]{0:T(256)S(1)}, f32[137]{0:T(256)}, u32[]{:S(2)}) copy-start(f32[137]{0:T(256)} %param.13) | copy-start | bytes 1648
  33.1 177.8 %all-to-all-start = ((bf16[80,128,274]{2,0,1:T(8,128)(2,1)}), bf16[80,128,274]{2,0,1:T(8,128)(2,1)}, u32[]{:S(2)}, u32[]{:S(2)}) async-start(bf16[80,128,274]{2,0,1:T(8,128)(2,1)} %select_convert_fusion.1), calls=%async_computation | async-start | bytes 15728640 | tf_op jit(solution)/shard_map/all_to_all | solution.py:36
  299.7 18.9 %copy-start.3 = (bf16[137,137]{1,0:T(8,128)(2,1)S(1)}, bf16[137,137]{1,0:T(8,128)(2,1)}, u32[]{:S(2)}) copy-start(bf16[137,137]{1,0:T(8,128)(2,1)} %param.15) | copy-start | bytes 112618
  369.4 17.6 %copy-start.2 = (bf16[1280,8,274]{0,2,1:T(8,128)(2,1)S(1)}, bf16[1280,8,274]{0,2,1:T(8,128)(2,1)}, u32[]{:S(2)}) copy-start(bf16[1280,8,274]{0,2,1:T(8,128)(2,1)} %fusion) | copy-start | bytes 16834564
  409.7 175.9 %all-to-all-start.1 = ((bf16[16,80,8,274]{3,2,1,0:T(8,128)(2,1)}), bf16[16,80,8,274]{3,2,1,0:T(8,128)(2,1)}, u32[]{:S(2)}, u32[]{:S(2)}) async-start(bf16[16,80,8,274]{3,2,1,0:T(8,128)(2,1)} %copy.50), calls=%async_computation.1 | async-start | bytes 15728640 | tf_op jit(solution)/shard_map/all_to_all | solution.py:44
  585.6 17.9 %copy-start.1 = (bf16[137,137]{1,0:T(8,128)(2,1)S(1)}, bf16[137,137]{1,0:T(8,128)(2,1)}, u32[]{:S(2)}) copy-start(bf16[137,137]{1,0:T(8,128)(2,1)} %param.14) | copy-start | bytes 112618
